TPU v7x, 32 devices: a whole 2x2x4 slice. The times are simulated.
32 devices in a mesh: groups: 2 (over y), pfx: 4 (over z), smp: 2 (over x), kv: 2 (over core).
Axes of the slice: x: 2, y: 2, z: 4, core: 2. Of those that a mesh axis runs over, the one named last changes fastest.
Arguments:
- hidden: bfloat16 [64, 8192], P(('groups', 'smp'), 'pfx'), parts along dimension 0, may hold values from -6 to 6
- norm_gain: bfloat16 [8192], P('pfx'), may hold values from 0.5 to 1.5
- query_weight: bfloat16 [8192, 4096], P('pfx', 'kv'), may hold values from -0.0625 to 0.0625
- key_matrix: bfloat16 [8192, 512], P('pfx', 'kv'), may hold values from -0.52734375 to 0.52734375
- value_matrix: bfloat16 [8192, 512], P('pfx', 'kv'), may hold values from -0.0625 to 0.0625
- prefix_key: bfloat16 [16384, 512], P(('groups', 'pfx', 'smp'), 'kv'), parts along dimension 0, may hold values from -160 to 160
- shared_prefix_value: bfloat16 [16384, 512], P(('groups', 'pfx', 'smp'), 'kv'), parts along dimension 0, may hold values from -6 to 6
- sample_suffix_key: bfloat16 [64, 128, 512], P(('groups', 'smp'), 'pfx', 'kv'), parts along dimension 0, may hold values from -24 to 24
- sample_suffix_value: bfloat16 [64, 128, 512], P(('groups', 'smp'), 'pfx', 'kv'), parts along dimension 0, may hold values from -6 to 6
- lengths: int32 [64], P(('groups', 'smp')), parts along dimension 0, may hold values from 1 to 128, as said below
- assign: int32 [64], P(('groups', 'smp')), parts along dimension 0, may hold values from 0 to 31, as said below
Outputs:
- attended: bfloat16 [64, 4096], P(('groups', 'smp'), 'kv'), parts along dimension 0
There are 2 independent parts, one for each index of `groups`. A program takes and returns all parts, laid end to end along the dimension named above; an argument that names none is the same for every part. Nothing has to cross between parts.
Inputs may be any that keep to these rules, and one draw needn't show every extreme that they name: `lengths`: some sample has exactly 128 live positions. `assign`: each aligned block of 16 rows holds each sample number of that block once.
All inputs are finite; a program needn't handle non-finite values.
Results may differ from a plain program's by a relative error of at most 0.017.
Values may be sent and summed in bfloat16 or wider, within the bound.
No kernel may reach another device: no remote copies, remote signals or barrier semaphores. Data moves between devices by JAX's collectives and lax.ppermute only.
A program may use at most 64 MiB of HBM per device.

v0:
```python
import jax
import jax.numpy as jnp
from jax import lax
from jax.sharding import PartitionSpec as P

MODEL_WIDTH = 8192
HEAD_WIDTH = 128
norm_eps = 1e-05
very_negative = -1e30


def prefix_head(operands):
    query_block, key_block, value_block = operands
    scores = jnp.einsum(
        "bgd,kd->bgk", query_block, key_block, preferred_element_type=jnp.float32
    ) * HEAD_WIDTH ** (-0.5)
    top_score = jnp.max(scores, axis=2)
    weights = jnp.exp(scores - top_score[..., None]).astype(jnp.bfloat16)
    denominator = jnp.sum(weights.astype(jnp.float32), axis=2)
    numerator = jnp.einsum("bgk,kd->bgd", weights, value_block, preferred_element_type=jnp.float32)
    return (numerator, denominator, top_score)


def body(
    hidden,
    norm_gain,
    query_weight,
    key_matrix,
    value_matrix,
    prefix_key,
    shared_prefix_value,
    sample_suffix_key,
    sample_suffix_value,
    lengths,
    assign,
):
    local_rows = hidden.shape[0]
    local_kv = key_matrix.shape[1] // HEAD_WIDTH
    local_heads = query_weight.shape[1] // HEAD_WIDTH
    group_width = local_heads // local_kv
    score_scale = HEAD_WIDTH ** (-0.5)
    hidden_wide = hidden.astype(jnp.float32)
    normed = (hidden_wide * norm_gain.astype(jnp.float32)).astype(jnp.bfloat16)
    query_part = jnp.dot(normed, query_weight, preferred_element_type=jnp.float32)
    key_part = jnp.dot(normed, key_matrix, preferred_element_type=jnp.float32)
    value_part = jnp.dot(normed, value_matrix, preferred_element_type=jnp.float32)
    square_part = jnp.sum(hidden_wide * hidden_wide, axis=1)
    query_sum, key_sum, value_sum, square_sum = lax.psum(
        (query_part, key_part, value_part, square_part), "pfx"
    )
    rms_value = jnp.sqrt(square_sum / MODEL_WIDTH + norm_eps)
    query_rows = (query_sum / rms_value[:, None]).astype(jnp.bfloat16)
    new_key = (key_sum / rms_value[:, None]).astype(jnp.bfloat16)
    new_value = (value_sum / rms_value[:, None]).astype(jnp.bfloat16)
    all_queries = lax.all_gather(query_rows, "smp", axis=0, tiled=True)
    sample_count = all_queries.shape[0]
    head_queries = jnp.transpose(
        all_queries.reshape(sample_count, local_kv, group_width, HEAD_WIDTH), (1, 0, 2, 3)
    )
    head_keys = jnp.transpose(prefix_key.reshape(-1, local_kv, HEAD_WIDTH), (1, 0, 2))
    head_values = jnp.transpose(shared_prefix_value.reshape(-1, local_kv, HEAD_WIDTH), (1, 0, 2))
    pre_numer, pre_denom, pre_top = lax.map(prefix_head, (head_queries, head_keys, head_values))
    pre_numer = jnp.transpose(pre_numer, (1, 0, 2, 3)).reshape(
        sample_count, local_heads, HEAD_WIDTH
    )
    pre_denom = jnp.transpose(pre_denom, (1, 0, 2)).reshape(sample_count, local_heads)
    pre_top = jnp.transpose(pre_top, (1, 0, 2)).reshape(sample_count, local_heads)
    row_base = lax.axis_index("smp") * local_rows
    slot_index = assign - row_base
    one_hot = (slot_index[:, None] == jnp.arange(local_rows, dtype=jnp.int32)[None, :]).astype(
        jnp.float32
    )
    slot_query = jnp.einsum(
        "rs,rx->sx", one_hot, query_rows.astype(jnp.float32), precision=lax.Precision.HIGHEST
    ).astype(jnp.bfloat16)
    slot_query = slot_query.reshape(local_rows, local_kv, group_width, HEAD_WIDTH)
    suffix_len = sample_suffix_key.shape[1]
    suffix_keys = sample_suffix_key.reshape(local_rows, suffix_len, local_kv, HEAD_WIDTH)
    suffix_values = sample_suffix_value.reshape(local_rows, suffix_len, local_kv, HEAD_WIDTH)
    suffix_scores = (
        jnp.einsum("shgd,sthd->shgt", slot_query, suffix_keys, preferred_element_type=jnp.float32)
        * score_scale
    )
    position = lax.axis_index("pfx") * suffix_len + jnp.arange(suffix_len, dtype=jnp.int32)
    live_mask = (position[None, :] < lengths[:, None])[:, None, None, :]
    suffix_scores = jnp.where(live_mask, suffix_scores, very_negative)
    suffix_top = jnp.max(suffix_scores, axis=3)
    suffix_weights = jnp.where(
        live_mask, jnp.exp(suffix_scores - suffix_top[..., None]), 0.0
    ).astype(jnp.bfloat16)
    suffix_denom = jnp.sum(suffix_weights.astype(jnp.float32), axis=3)
    suffix_numer = jnp.einsum(
        "shgt,sthd->shgd", suffix_weights, suffix_values, preferred_element_type=jnp.float32
    )
    row_numer = jnp.einsum(
        "rs,shgd->rhgd", one_hot, suffix_numer, precision=lax.Precision.HIGHEST
    ).reshape(local_rows, local_heads, HEAD_WIDTH)
    row_denom = jnp.einsum(
        "rs,shg->rhg", one_hot, suffix_denom, precision=lax.Precision.HIGHEST
    ).reshape(local_rows, local_heads)
    row_top = jnp.einsum(
        "rs,shg->rhg", one_hot, suffix_top, precision=lax.Precision.HIGHEST
    ).reshape(local_rows, local_heads)
    full_top = lax.dynamic_update_slice(
        jnp.full((sample_count, local_heads), very_negative, jnp.float32), row_top, (row_base, 0)
    )
    local_top = jnp.maximum(pre_top, full_top)
    global_top = lax.pmax(local_top, ("pfx", "smp"))
    own_top = lax.dynamic_slice_in_dim(global_top, row_base, local_rows, 0)
    pre_factor = jnp.exp(pre_top - global_top)
    row_factor = jnp.exp(row_top - own_top)
    scaled_row_numer = row_numer * row_factor[..., None]
    scaled_row_denom = row_denom * row_factor
    term_numer = pre_numer * pre_factor[..., None]
    term_denom = pre_denom * pre_factor
    term_numer = lax.dynamic_update_slice(
        term_numer,
        lax.dynamic_slice_in_dim(term_numer, row_base, local_rows, 0) + scaled_row_numer,
        (row_base, 0, 0),
    )
    term_denom = lax.dynamic_update_slice(
        term_denom,
        lax.dynamic_slice_in_dim(term_denom, row_base, local_rows, 0) + scaled_row_denom,
        (row_base, 0),
    )
    block_numer, block_denom = (
        lax.psum_scatter(
            term_numer.astype(jnp.bfloat16), "smp", scatter_dimension=0, tiled=True
        ).astype(jnp.float32),
        lax.psum_scatter(
            term_denom.astype(jnp.bfloat16), "smp", scatter_dimension=0, tiled=True
        ).astype(jnp.float32),
    )
    numerator, denominator = (
        lax.psum(block_numer.astype(jnp.bfloat16), "pfx").astype(jnp.float32),
        lax.psum(block_denom.astype(jnp.bfloat16), "pfx").astype(jnp.float32),
    )
    query_wide = query_rows.reshape(local_rows, local_kv, group_width, HEAD_WIDTH).astype(
        jnp.float32
    )
    own_key = new_key.reshape(local_rows, local_kv, 1, HEAD_WIDTH).astype(jnp.float32)
    own_score = (jnp.sum(query_wide * own_key, axis=3) * score_scale).reshape(
        local_rows, local_heads
    )
    final_top = jnp.maximum(own_top, own_score)
    old_factor = jnp.exp(own_top - final_top)
    own_weight = lax.optimization_barrier(
        jnp.exp(own_score - final_top).astype(jnp.bfloat16)
    ).astype(jnp.float32)
    own_value = jnp.broadcast_to(
        new_value.reshape(local_rows, local_kv, 1, HEAD_WIDTH).astype(jnp.float32),
        (local_rows, local_kv, group_width, HEAD_WIDTH),
    ).reshape(local_rows, local_heads, HEAD_WIDTH)
    numerator = numerator * old_factor[..., None] + own_weight[..., None] * own_value
    denominator = denominator * old_factor + own_weight
    return (
        (numerator / denominator[..., None])
        .astype(jnp.bfloat16)
        .reshape(local_rows, local_heads * HEAD_WIDTH)
    )


def solution(mesh):
    return jax.shard_map(
        body,
        mesh=mesh,
        in_specs=(
            P(("groups", "smp"), "pfx"),
            P("pfx"),
            P("pfx", "kv"),
            P("pfx", "kv"),
            P("pfx", "kv"),
            P(("groups", "pfx", "smp"), "kv"),
            P(("groups", "pfx", "smp"), "kv"),
            P(("groups", "smp"), "pfx", "kv"),
            P(("groups", "smp"), "pfx", "kv"),
            P(("groups", "smp")),
            P(("groups", "smp")),
        ),
        out_specs=P(("groups", "smp"), "kv"),
        check_vma=False,
    )
```

profile of v0, /device:TPU:0, one launch (start us, length us, event | category | flops | bytes accessed | tf_op | source)
XLA Modules:
  0.0 151.5 jit_solution(18185746916683848563)
XLA Ops:
  6.5 0.8 convert_element_type.89
  7.4 5.4 %fusion.30 = f32[16,2048]{1,0:T(8,128)} fusion(bf16[2048,2048]{1,0:T(8,128)(2,1)} %param.15, bf16[16,2048]{1,0:T(8,128)(2,1)} %param.13, f32[2048]{0:T(1024)S(1)} %convert_element_type.89), kind=kOutput, calls=%fused_computation.49 | convolution fusion | flops 134316032 | bytes 8593408 | tf_op jit(solution)/shard_map/dot_general | solution.py:44
  12.9 0.1 fusion.18
  13.0 0.5 iota_add_fusion
  13.5 0.2 fusion.28
  13.8 0.3 fusion.26
  14.0 21.5 %all-reduce = (f32[16]{0:T(128)S(1)}, f32[16,256]{1,0:T(8,128)S(1)}, f32[16,256]{1,0:T(8,128)S(1)}) all-reduce(f32[16]{0:T(128)S(1)} %fusion.18, f32[16,256]{1,0:T(8,128)S(1)} %fusion.28, f32[16,256]{1,0:T(8,128)S(1)} %fusion.26), channel_id=1, replica_groups=mesh['groups'=2,'pfx'=4,'smp'=2,'kv'=2] {'pfx'}, use_global_device_ids=true, to_apply=%region_2.0 | all-reduce | flops 8208 | bytes 65664 | tf_op jit(solution)/shard_map/psum | solution.py:48
  35.7 0.2 copy.55
  35.9 0.2 copy.56
  36.1 0.7 broadcast_compare_fusion
  36.8 0.7 broadcast_subtract_fusion
  37.4 13.1 %all-reduce.4.cloned.1.call-done = f32[16,2048]{1,0:T(8,128)} async-done(((f32[16,2048]{1,0:T(8,128)}), f32[16,2048]{1,0:T(8,128)}) %all-reduce.4.cloned.1.call-update) | async-done | bytes 131088 | tf_op jit(solution)/shard_map/psum | solution.py:48
  50.5 1.0 convert_bitcast_fusion
  51.5 0.1 multiply_reduce_fusion
  51.7 4.9 %all_gather.3 = bf16[32,2048]{1,0:T(8,128)(2,1)S(1)} all-gather(bf16[16,2048]{1,0:T(8,128)(2,1)S(1)} %get-tuple-element.97), channel_id=1, replica_groups=mesh['groups'=2,'pfx'=4,'smp'=2,'kv'=2] {'smp'}, dimensions={0}, use_global_device_ids=true | all-gather | bytes 196608 | tf_op jit(solution)/shard_map/all_gather | solution.py:55
  56.7 0.3 fusion.10
  57.0 0.3 fusion.51
  57.4 0.2 fusion.38
  57.6 0.2 convert_reduce_fusion.1
  57.9 1.2 fusion.12
  59.1 0.3 fusion.24
  59.4 4.6 %while.14 = (s32[]{:T(128)}, f32[2,32,8,128]{3,2,0,1:T(8,128)}, f32[2,32,8]{2,1,0:T(8,128)}, f32[2,32,8]{2,1,0:T(8,128)S(1)}, bf16[2,32,8,128]{3,2,1,0:T(8,128)(...) while((s32[]{:T(128)}, f32[2,32,8,128]{3,2,0,1:T(8,128)}, ...), condition=%wide.region_6.7_spmd, body=%wide.region_3.6_spmd.sunk | while | flops 136314368 | bytes 3953761 | solution.py:62
  59.4 0.4 fusion.63
  59.8 0.3 convert_reduce_fusion.3
  60.1 1.0 fusion.64
  61.1 0.6 bitcast_dynamic-update-slice_fusion.3
  61.7 0.4 fusion.63
  62.1 0.3 convert_reduce_fusion.3
  62.4 1.0 fusion.64
  63.4 0.6 bitcast_dynamic-update-slice_fusion.3
  64.1 0.2 dynamic_update_slice.20
  64.3 20.4 %pmax.7 = f32[32,16]{0,1:T(8,128)S(1)} all-reduce(f32[32,16]{0,1:T(8,128)S(1)} %bitcast_maximum_fusion), channel_id=1, replica_groups=mesh['groups'=2,'pfx'=4,'smp'=2,'kv'=2] {'pfx','smp'}, use_global_device_ids=true, to_apply=%region_8.9 | all-reduce | flops 512 | bytes 4096 | tf_op jit(solution)/shard_map/pmax | solution.py:108
  84.7 0.1 fusion.34
  84.9 0.8 copy.71
  85.7 0.2 fusion.11
  85.9 0.2 dynamic_update_slice.22
  86.1 0.7 copy.75
  86.9 1.1 bitcast_multiply_fusion
  88.0 0.1 fusion.23
  88.1 0.7 convert_element_type.94
  88.9 5.2 %reduce-scatter.7.cloned.1.call-done = bf16[16,16]{1,0:T(8,128)(2,1)} async-done(((bf16[32,16]{1,0:T(8,128)(2,1)}), bf16[16,16]{1,0:T(8,128)(2,1)}) %reduce-scatter.7.cloned.1.call-update) | async-done | bytes 528
  94.2 0.7 copy.76
  94.9 11.7 %psum.47 = bf16[16,16]{0,1:T(8,128)(2,1)S(1)} all-reduce(bf16[16,16]{0,1:T(8,128)(2,1)S(1)} %copy.76), channel_id=1, replica_groups=mesh['groups'=2,'pfx'=4,'smp'=2,'kv'=2] {'pfx'}, use_global_device_ids=true, to_apply=%region_16.17 | all-reduce | flops 256 | bytes 1024 | tf_op jit(solution)/shard_map/psum | solution.py:136
  106.6 0.2 reduce-scatter.5.cloned.1.call-done
  106.8 0.1 multiply_add_fusion
  107.0 36.3 %all-reduce.6.cloned.1.call-done = bf16[16,16,128]{2,1,0:T(8,128)(2,1)} async-done(((bf16[16,16,128]{2,1,0:T(8,128)(2,1)}), bf16[16,16,128]{2,1,0:T(8,128)(2,1)}) %all-reduce.6.cloned.1.call-update) | async-done | bytes 65552 | tf_op jit(solution)/shard_map/psum | solution.py:135
  143.3 1.0 fusion.21
  144.3 0.6 copy.110
  (46 shorter events, 1.1 us)
Async XLA Ops:
  6.5 7.0 %copy-start = (bf16[2048,256]{1,0:T(8,128)(2,1)S(1)}, bf16[2048,256]{1,0:T(8,128)(2,1)}, u32[]{:S(2)}) copy-start(bf16[2048,256]{1,0:T(8,128)(2,1)} %param.16) | copy-start | bytes 3145732
  6.5 6.3 %copy-start.1 = (bf16[16,2048]{1,0:T(8,128)(2,1)S(1)}, bf16[16,2048]{1,0:T(8,128)(2,1)}, u32[]{:S(2)}) copy-start(bf16[16,2048]{1,0:T(8,128)(2,1)} %param.13) | copy-start | bytes 196612
  6.5 44.0 %all-reduce.4.cloned.1.call-start = ((), (), s32[]{:S(2)}) async-start(), calls=%async_computation.2 | async-start | bytes 262144 | tf_op jit(solution)/shard_map/psum | solution.py:48
  7.3 6.5 %copy-start.2 = (bf16[2048,256]{1,0:T(8,128)(2,1)S(1)}, bf16[2048,256]{1,0:T(8,128)(2,1)}, u32[]{:S(2)}) copy-start(bf16[2048,256]{1,0:T(8,128)(2,1)} %param.17) | copy-start | bytes 3145732
  7.3 28.3 %copy-start.3 = (bf16[1024,256]{1,0:T(8,128)(2,1)S(1)}, bf16[1024,256]{1,0:T(8,128)(2,1)}, u32[]{:S(2)}) copy-start(bf16[1024,256]{1,0:T(8,128)(2,1)} %param.18) | copy-start | bytes 1572868
  7.3 28.5 %copy-start.4 = (bf16[1024,256]{1,0:T(8,128)(2,1)S(1)}, bf16[1024,256]{1,0:T(8,128)(2,1)}, u32[]{:S(2)}) copy-start(bf16[1024,256]{1,0:T(8,128)(2,1)} %param.19) | copy-start | bytes 1572868
  7.3 28.8 %copy-start.6 = (s32[16]{0:T(128)S(1)}, s32[16]{0:T(128)}, u32[]{:S(2)}) copy-start(s32[16]{0:T(128)} %param.22) | copy-start | bytes 196
  7.3 49.7 %copy-start.5 = (bf16[16,32,256]{2,1,0:T(8,128)(2,1)S(1)}, bf16[16,32,256]{2,1,0:T(8,128)(2,1)}, u32[]{:S(2)}) copy-start(bf16[16,32,256]{2,1,0:T(8,128)(2,1)} %param.20) | copy-start | bytes 786436
  12.8 81.4 %reduce-scatter.7.cloned.1.call-start = ((), (), s32[]{:S(2)}) async-start(), calls=%async_computation.5 | async-start | bytes 12288
  86.8 20.0 %reduce-scatter.5.cloned.1.call-start = ((), (), s32[]{:S(2)}) async-start(), calls=%async_computation.3 | async-start | bytes 196608 | tf_op jit(solution)/shard_map/reduce_scatter | solution.py:127
  88.8 54.5 %all-reduce.6.cloned.1.call-start = ((), (), s32[]{:S(2)}) async-start(), calls=%async_computation.4 | async-start | bytes 131072 | tf_op jit(solution)/shard_map/psum | solution.py:135
Sparse Core Ops, SparseCore 0:
  12.9 37.5 all-reduce.3
  86.9 7.2 reduce-scatter.6
  96.4 10.3 reduce-scatter.4
  109.0 34.2 all-reduce.5
where the time goes:
time: 152 us; the launch traced here: 151 us
  blocking collectives  58.5 us (38%)
  waiting for transfers between devices  54.8 us (36%)
  between operations  13.4 us (9%)
  matrix products  11.1 us (7%)
  other arithmetic  7.82 us (5%)
  local copies, waits for them, and re-layouts  5.69 us (4%)
    psum x1, waiting for transfers between devices, body(): lax.psum(block_numer.astype(jnp.bfloat16), 'pfx').astype(jnp.float32)  36.3 us
    psum x1, blocking collectives, body(): lax.psum((query_part, key_part, value_part, square_part), 'pfx')  21.5 us
    pmax x1, blocking collectives, body(): global_top = lax.pmax(local_top, ('pfx', 'smp'))  20.4 us
    psum x1, waiting for transfers between devices, body(): lax.psum((query_part, key_part, value_part, square_part), 'pfx')  13.1 us
    psum x1, blocking collectives, body(): lax.psum(block_denom.astype(jnp.bfloat16), 'pfx').astype(jnp.float32)  11.7 us
    dot_general x1, matrix products, body(): jnp.dot(normed, query_weight, preferred_element_type=jnp.float32)  5.42 us
    unnamed x5, waiting for transfers between devices  5.3 us
    all_gather x1, blocking collectives, body(): all_queries = lax.all_gather(query_rows, 'smp', axis=0, tiled=True)  4.93 us
  transfers between devices with their start and end apart: 4, of which 4 were waited for; matrix products, arithmetic and copies ran while one was open for 4% of the time, Pallas kernels for 0%

commit v1 on v0

--- a/solution.py
+++ b/solution.py
@@ -132,7 +132,9 @@
         ).astype(jnp.float32),
     )
     numerator, denominator = (
-        lax.psum(block_numer.astype(jnp.bfloat16), "pfx").astype(jnp.float32),
+        jnp.sum(lax.all_gather(block_numer.astype(jnp.bfloat16), "pfx"), axis=0).astype(
+            jnp.float32
+        ),
         lax.psum(block_denom.astype(jnp.bfloat16), "pfx").astype(jnp.float32),
     )
     query_wide = query_rows.reshape(local_rows, local_kv, group_width, HEAD_WIDTH).astype(

time: 152 us -> 126 us (0.83)
  waiting for transfers between devices: 54.8 us -> 19.7 us
  blocking collectives: 58.5 us -> 72.8 us
  matrix products: 11.1 us -> 8.86 us
  other arithmetic: 7.82 us -> 5.68 us
    psum x1 -> x0, waiting for transfers between devices: 36.3 us -> none  [body(): lax.psum(block_numer.astype(jnp.bfloat16), 'pfx').astype(jnp.float32)]
    all_gather x0 -> x1, blocking collectives: none -> 14 us  [body(): lax.all_gather(block_numer.astype(jnp.bfloat16), 'pfx')]
    unnamed x5 -> x4, waiting for transfers between devices: 5.3 us -> 5.7 us
  transfers between devices with their start and end apart: 4 -> 3, of which waited for: 4 -> 2; matrix products, arithmetic and copies ran while one was open for 4% -> 4% of each run, Pallas kernels for 0% -> 0%
where the time goes in v1:
time: 126 us
  blocking collectives  72.8 us (58%)
  waiting for transfers between devices  19.7 us (16%)
  between operations  13.4 us (11%)
  matrix products  8.86 us (7%)
  other arithmetic  5.68 us (5%)
  local copies, waits for them, and re-layouts  5.25 us (4%)
    psum x1, blocking collectives, body(): lax.psum((query_part, key_part, value_part, square_part), 'pfx')  21.7 us
    pmax x1, blocking collectives, body(): global_top = lax.pmax(local_top, ('pfx', 'smp'))  20.4 us
    all_gather x1, blocking collectives, body(): lax.all_gather(block_numer.astype(jnp.bfloat16), 'pfx')  14 us
    psum x1, waiting for transfers between devices, body(): lax.psum((query_part, key_part, value_part, square_part), 'pfx')  14 us
    psum x1, blocking collectives, body(): lax.psum(block_denom.astype(jnp.bfloat16), 'pfx').astype(jnp.float32)  11.7 us
    unnamed x4, waiting for transfers between devices  5.7 us
    dot_general x1, matrix products, body(): jnp.dot(normed, query_weight, preferred_element_type=jnp.float32)  5.42 us
    all_gather x1, blocking collectives, body(): all_queries = lax.all_gather(query_rows, 'smp', axis=0, tiled=True)  4.93 us
  transfers between devices with their start and end apart: 3, of which 2 were waited for; matrix products, arithmetic and copies ran while one was open for 4% of the time, Pallas kernels for 0%

profile of v1, /device:TPU:0, one launch (start us, length us, event | category | flops | bytes accessed | tf_op | source)
XLA Modules:
  0.0 125.7 jit_solution(7860392374723255618)
XLA Ops:
  6.5 0.8 convert_element_type.94
  7.3 5.4 %fusion.29 = f32[16,2048]{1,0:T(8,128)} fusion(bf16[2048,2048]{1,0:T(8,128)(2,1)} %param.15, bf16[16,2048]{1,0:T(8,128)(2,1)} %param.13, f32[2048]{0:T(1024)S(1)} %convert_element_type.94), kind=kOutput, calls=%fused_computation.49 | convolution fusion | flops 134316032 | bytes 8593408 | tf_op jit(solution)/shard_map/dot_general | solution.py:44
  12.9 0.1 fusion.18
  13.0 0.2 fusion.27
  13.3 0.3 fusion.25
  13.5 21.7 %all-reduce = (f32[16]{0:T(128)S(1)}, f32[16,256]{1,0:T(8,128)S(1)}, f32[16,256]{1,0:T(8,128)S(1)}) all-reduce(f32[16]{0:T(128)S(1)} %fusion.18, f32[16,256]{1,0:T(8,128)S(1)} %fusion.27, f32[16,256]{1,0:T(8,128)S(1)} %fusion.25), channel_id=1, replica_groups=mesh['groups'=2,'pfx'=4,'smp'=2,'kv'=2] {'pfx'}, use_global_device_ids=true, to_apply=%region_2.0 | all-reduce | flops 8208 | bytes 65664 | tf_op jit(solution)/shard_map/psum | solution.py:48
  35.3 0.2 copy.56
  35.5 0.2 copy.57
  35.7 0.1 fusion.35
  35.9 0.7 broadcast_subtract_fusion
  36.5 14.0 %all-reduce.3.cloned.1.call-done = f32[16,2048]{1,0:T(8,128)} async-done(((f32[16,2048]{1,0:T(8,128)}), f32[16,2048]{1,0:T(8,128)}) %all-reduce.3.cloned.1.call-update) | async-done | bytes 131088 | tf_op jit(solution)/shard_map/psum | solution.py:48
  50.5 1.0 convert_bitcast_fusion
  51.5 4.9 %all_gather.9 = bf16[32,2048]{1,0:T(8,128)(2,1)S(1)} all-gather(bf16[16,2048]{1,0:T(8,128)(2,1)S(1)} %get-tuple-element.97), channel_id=1, replica_groups=mesh['groups'=2,'pfx'=4,'smp'=2,'kv'=2] {'smp'}, dimensions={0}, use_global_device_ids=true | all-gather | bytes 196608 | tf_op jit(solution)/shard_map/all_gather | solution.py:55
  56.5 3.3 %while.14 = (s32[]{:T(128)}, f32[2,32,8,128]{3,2,0,1:T(8,128)S(1)}, f32[2,32,8]{2,1,0:T(8,128)S(1)}, f32[2,32,8]{2,1,0:T(8,128)}, bf16[2,32,8,128]{3,2,1,0:T(8,1...) while((s32[]{:T(128)}, f32[2,32,8,128]{3,2,0,1:T(8,128)S(1)}, ...), condition=%wide.region_6.7_spmd, body=%wide.region_3.6_spmd.sunk | while | flops 136314368 | bytes 3953761 | solution.py:62
  56.5 0.4 fusion.62
  56.9 0.3 fusion.63
  57.3 0.3 convert_reduce_fusion.3
  57.6 0.6 bitcast_dynamic-update-slice_fusion.3
  58.2 0.4 fusion.62
  58.6 0.4 fusion.63
  58.9 0.3 convert_reduce_fusion.3
  59.2 0.6 bitcast_dynamic-update-slice_fusion.3
  59.9 0.3 fusion.10
  60.2 0.3 fusion.50
  60.6 0.2 fusion.37
  60.8 0.8 copy.61
  61.7 0.2 dynamic_update_slice.20
  61.8 20.4 %pmax.7 = f32[32,16]{0,1:T(8,128)S(1)} all-reduce(f32[32,16]{0,1:T(8,128)S(1)} %bitcast_maximum_fusion), channel_id=1, replica_groups=mesh['groups'=2,'pfx'=4,'smp'=2,'kv'=2] {'pfx','smp'}, use_global_device_ids=true, to_apply=%region_8.9 | all-reduce | flops 512 | bytes 4096 | tf_op jit(solution)/shard_map/pmax | solution.py:108
  82.3 0.1 multiply_reduce_fusion
  82.5 0.1 fusion.33
  82.6 0.2 convert_reduce_fusion.1
  83.0 0.2 fusion.11
  83.2 0.2 dynamic_update_slice.22
  83.4 0.7 copy.76
  84.2 0.2 fusion.12
  84.4 0.3 fusion.23
  84.7 0.1 bitcast_multiply_fusion
  84.9 0.1 fusion.22
  85.0 0.7 convert_element_type.99
  85.7 5.7 %reduce-scatter.7.cloned.1.call-done = bf16[16,16]{1,0:T(8,128)(2,1)} async-done(((bf16[32,16]{1,0:T(8,128)(2,1)}), bf16[16,16]{1,0:T(8,128)(2,1)}) %reduce-scatter.7.cloned.1.call-update) | async-done | bytes 528
  91.4 0.7 copy.77
  92.1 11.7 %psum.39 = bf16[16,16]{0,1:T(8,128)(2,1)S(1)} all-reduce(bf16[16,16]{0,1:T(8,128)(2,1)S(1)} %copy.77), channel_id=1, replica_groups=mesh['groups'=2,'pfx'=4,'smp'=2,'kv'=2] {'pfx'}, use_global_device_ids=true, to_apply=%region_16.17 | all-reduce | flops 256 | bytes 1024 | tf_op jit(solution)/shard_map/psum | solution.py:138
  103.8 0.1 multiply_add_fusion
  104.0 14.0 %all-gather = bf16[64,16,128]{2,1,0:T(8,128)(2,1)S(1)} all-gather(bf16[16,16,128]{2,1,0:T(8,128)(2,1)} %reduce-scatter.5.cloned.1.call-done), channel_id=2, replica_groups=mesh['groups'=2,'pfx'=4,'smp'=2,'kv'=2] {'pfx'}, dimensions={0}, use_global_device_ids=true | all-gather | bytes 327680 | tf_op jit(solution)/shard_map/all_gather | solution.py:135
  118.1 0.1 convert_multiply_fusion.2
  118.2 0.1 div.42
  118.3 0.1 mul.111
  118.4 0.8 fusion.19
  (50 shorter events, 1.1 us)
Async XLA Ops:
  6.5 6.5 %copy-start = (bf16[2048,256]{1,0:T(8,128)(2,1)S(1)}, bf16[2048,256]{1,0:T(8,128)(2,1)}, u32[]{:S(2)}) copy-start(bf16[2048,256]{1,0:T(8,128)(2,1)} %param.16) | copy-start | bytes 3145732
  6.5 6.3 %copy-start.1 = (bf16[16,2048]{1,0:T(8,128)(2,1)S(1)}, bf16[16,2048]{1,0:T(8,128)(2,1)}, u32[]{:S(2)}) copy-start(bf16[16,2048]{1,0:T(8,128)(2,1)} %param.13) | copy-start | bytes 196612
  6.5 44.0 %all-reduce.3.cloned.1.call-start = ((), (), s32[]{:S(2)}) async-start(), calls=%async_computation.2 | async-start | bytes 262144 | tf_op jit(solution)/shard_map/psum | solution.py:48
  7.3 5.9 %copy-start.2 = (bf16[2048,256]{1,0:T(8,128)(2,1)S(1)}, bf16[2048,256]{1,0:T(8,128)(2,1)}, u32[]{:S(2)}) copy-start(bf16[2048,256]{1,0:T(8,128)(2,1)} %param.17) | copy-start | bytes 3145732
  7.3 27.9 %copy-start.3 = (bf16[1024,256]{1,0:T(8,128)(2,1)S(1)}, bf16[1024,256]{1,0:T(8,128)(2,1)}, u32[]{:S(2)}) copy-start(bf16[1024,256]{1,0:T(8,128)(2,1)} %param.18) | copy-start | bytes 1572868
  7.3 28.1 %copy-start.4 = (bf16[1024,256]{1,0:T(8,128)(2,1)S(1)}, bf16[1024,256]{1,0:T(8,128)(2,1)}, u32[]{:S(2)}) copy-start(bf16[1024,256]{1,0:T(8,128)(2,1)} %param.19) | copy-start | bytes 1572868
  7.3 28.5 %copy-start.6 = (s32[16]{0:T(128)S(1)}, s32[16]{0:T(128)}, u32[]{:S(2)}) copy-start(s32[16]{0:T(128)} %param.22) | copy-start | bytes 196
  12.8 78.6 %reduce-scatter.7.cloned.1.call-start = ((), (), s32[]{:S(2)}) async-start(), calls=%async_computation.4 | async-start | bytes 12288
  56.5 3.7 %copy-start.5 = (bf16[16,32,256]{2,1,0:T(8,128)(2,1)S(1)}, bf16[16,32,256]{2,1,0:T(8,128)(2,1)}, u32[]{:S(2)}) copy-start(bf16[16,32,256]{2,1,0:T(8,128)(2,1)} %param.20) | copy-start | bytes 786436
  56.5 27.7 %copy-start.7 = (bf16[16,32,256]{2,1,0:T(8,128)(2,1)S(1)}, bf16[16,32,256]{2,1,0:T(8,128)(2,1)}, u32[]{:S(2)}) copy-start(bf16[16,32,256]{2,1,0:T(8,128)(2,1)} %param.21) | copy-start | bytes 786436
  84.1 20.0 %reduce-scatter.5.cloned.1.call-start = ((), (), s32[]{:S(2)}) async-start(), calls=%async_computation.3 | async-start | bytes 196608 | tf_op jit(solution)/shard_map/reduce_scatter | solution.py:127
Sparse Core Ops, SparseCore 0:
  12.9 37.5 all-reduce.2
  84.2 7.1 reduce-scatter.6
  93.6 10.3 reduce-scatter.4
